TPU v7x, 512 devices: a whole 4x8x8 slice. The times are simulated.
512 devices in a mesh: round: 128 (over z, y, core), mp: 4 (over x).
Axes of the slice: x: 4, y: 8, z: 8, core: 2. Of those that a mesh axis runs over, the one named last changes fastest.
Arguments:
- tokens: bfloat16 [128, 512, 512], P('round'), may hold values from -8 to 8
- cell_order: int32 [512], replicated, may hold values from 0 to 511, each once
- seam_rows: int32 [128, 128, 2], P('round'), may hold values from -1 to 511, as said below
- obs_mask: int32 [16, 512], replicated, may hold values from 0 to 1, as said below
- norm_gain: float32 [512], replicated, may hold values from 0.1 to 1.9
- w_query: bfloat16 [512, 512], P(None, 'mp'), may hold values from -1 to 1
- w_key: bfloat16 [512, 512], P(None, 'mp'), may hold values from -1 to 1
- w_value: bfloat16 [512, 512], P(None, 'mp'), may hold values from -0.25 to 0.25
- w_out: bfloat16 [512, 512], P('mp'), may hold values from -0.25 to 0.25
- w_gate: bfloat16 [512, 2048], P(None, 'mp'), may hold values from -0.25 to 0.25
- w_up: bfloat16 [512, 2048], P(None, 'mp'), may hold values from -0.25 to 0.25
- w_down: bfloat16 [2048, 512], P('mp'), may hold values from -0.125 to 0.125
- w_read: float32 [512], replicated, may hold values from -0.25 to 0.25
Outputs:
- tiles_out: bfloat16 [128, 512, 512], P('mp', 'round')
- obs_logits: float32 [16], replicated
Inputs may be any that keep to these rules, and one draw needn't show every extreme that they name: `seam_rows`: each entry is a row of the sending tile or -1 for an empty slot; the live entries of one tile are all different; a tile's slots to itself are full, and some owner's slots are full from every tile. `obs_mask`: every observable's support holds at least one cell.
All inputs are finite; a program needn't handle non-finite values.
Results may differ from a plain program's by a relative error of at most 0.0052.
The roundings to bfloat16 on the way count: a program that leaves them out, or rounds other values in their place, can miss the bound.
Values may be sent and summed in bfloat16 or wider, within the bound.
A program may use at most 64 MiB of HBM per device.

v0:
```python
import math
import jax
import jax.numpy as jnp
from jax import lax
from jax.sharding import PartitionSpec as P

HDIM = 64
norm_eps = 1e-06


def normalize(rows_in, norm_gain):
    values = rows_in.astype(jnp.float32)
    spread = jnp.mean(values * values, axis=-1, keepdims=True)
    return (values * lax.rsqrt(spread + norm_eps) * norm_gain).astype(jnp.bfloat16)


def attend(queries, keys_all, values_all, live_keys):
    scale_factor = 1.0 / math.sqrt(queries.shape[-1])
    scores = (
        jnp.einsum("qhe,khe->hqk", queries, keys_all, preferred_element_type=jnp.float32)
        * scale_factor
    )
    if live_keys is not None:
        scores = jnp.where(live_keys[None, None, :], scores, -1e30)
    row_max = jnp.max(scores, axis=-1, keepdims=True)
    weights = jnp.exp(scores - row_max)
    probabilities = (weights / jnp.sum(weights, axis=-1, keepdims=True)).astype(jnp.bfloat16)
    mixture = jnp.einsum(
        "hqk,khe->qhe", probabilities, values_all, preferred_element_type=jnp.float32
    )
    return mixture.reshape(mixture.shape[0], -1)


def shards(
    tokens,
    cell_order,
    seam_rows,
    obs_mask,
    norm_gain,
    w_query,
    w_key,
    w_value,
    w_out,
    w_gate,
    w_up,
    w_down,
    w_read,
):
    round_count = lax.axis_size("round")
    model_count = lax.axis_size("mp")
    model_index = lax.axis_index("mp")
    round_index = lax.axis_index("round")
    width = tokens.shape[2]
    cell_dev = tokens.shape[1] // round_count
    permuted = tokens[:, cell_order, :]
    tile_tokens = lax.all_to_all(permuted, "round", split_axis=1, concat_axis=0, tiled=True)
    tile_rows = tile_tokens.shape[0] * cell_dev
    flat_tokens = tile_tokens.reshape(tile_rows, width)
    normed = normalize(flat_tokens, norm_gain)
    queries = jnp.dot(normed, w_query, preferred_element_type=jnp.float32).astype(jnp.bfloat16)
    keys_all = jnp.dot(normed, w_key, preferred_element_type=jnp.float32).astype(jnp.bfloat16)
    values_all = jnp.dot(normed, w_value, preferred_element_type=jnp.float32).astype(jnp.bfloat16)
    head_width = queries.shape[1]
    heads_dev = head_width // HDIM
    block_rows = min(512, tile_rows)
    query_blocks = queries.reshape(tile_rows // block_rows, block_rows, heads_dev, HDIM)
    key_heads = keys_all.reshape(tile_rows, heads_dev, HDIM)
    value_heads = values_all.reshape(tile_rows, heads_dev, HDIM)
    local_attn = lax.map(
        lambda query_block: attend(query_block, key_heads, value_heads, None), query_blocks
    )
    local_attn = local_attn.reshape(tile_rows, head_width)
    live_slot = seam_rows[0] >= 0
    safe_rows = jnp.where(live_slot, seam_rows[0], 0)
    packet = (
        lax.all_to_all(queries[safe_rows], "round", split_axis=0, concat_axis=0, tiled=True),
        lax.all_to_all(keys_all[safe_rows], "round", split_axis=0, concat_axis=0, tiled=True),
        lax.all_to_all(values_all[safe_rows], "round", split_axis=0, concat_axis=0, tiled=True),
        lax.all_to_all(
            live_slot.astype(jnp.bfloat16), "round", split_axis=0, concat_axis=0, tiled=True
        ),
    )
    seam_queries = packet[0].reshape(-1, heads_dev, HDIM)
    seam_keys = packet[1].reshape(-1, heads_dev, HDIM)
    seam_values = packet[2].reshape(-1, heads_dev, HDIM)
    seam_live = packet[3].reshape(-1) > 0.5
    seam_attn = attend(seam_queries, seam_keys, seam_values, seam_live).astype(jnp.bfloat16)
    returned = lax.all_to_all(
        seam_attn.reshape(round_count, -1, head_width),
        "round",
        split_axis=0,
        concat_axis=0,
        tiled=True,
    )
    target = jnp.where(live_slot, seam_rows[0], tile_rows).reshape(-1)
    combined = (
        local_attn.at[target]
        .add(returned.reshape(-1, head_width).astype(jnp.float32), mode="drop")
        .astype(jnp.bfloat16)
    )
    share_rows = tile_rows // model_count
    own_first = model_index * share_rows
    gate_part = jnp.dot(normed, w_gate, preferred_element_type=jnp.float32)
    up_part = jnp.dot(normed, w_up, preferred_element_type=jnp.float32)
    hidden = (jax.nn.silu(gate_part) * up_part).astype(jnp.bfloat16)
    attn_part = jnp.dot(combined, w_out, preferred_element_type=jnp.float32)
    summed = lax.psum_scatter(
        attn_part + jnp.dot(hidden, w_down, preferred_element_type=jnp.float32),
        "mp",
        scatter_dimension=0,
        tiled=True,
    )
    own_rows = lax.dynamic_slice_in_dim(flat_tokens, own_first, share_rows, 0)
    result_rows = (own_rows.astype(jnp.float32) + summed).astype(jnp.bfloat16)
    tiles_out = result_rows.reshape(share_rows // cell_dev, cell_dev, width)
    my_cells = lax.dynamic_slice_in_dim(cell_order, round_index * cell_dev, cell_dev)
    support = obs_mask[:, my_cells].astype(jnp.float32)
    partial_sum = jnp.einsum(
        "oc,rcd->od", support, tiles_out.astype(jnp.float32), precision=lax.Precision.HIGHEST
    )
    support_count = round_count * jnp.sum(obs_mask.astype(jnp.float32), axis=1)
    divisor = jnp.sqrt(support_count)
    pooled = lax.psum(partial_sum, ("round", "mp"))
    obs_logits = jnp.dot(pooled, w_read, precision=lax.Precision.HIGHEST) / divisor
    return (tiles_out, obs_logits)


def solution(mesh):
    return jax.shard_map(
        shards,
        mesh=mesh,
        in_specs=(
            P("round", None, None),
            P(),
            P("round", None, None),
            P(),
            P(),
            P(None, "mp"),
            P(None, "mp"),
            P(None, "mp"),
            P("mp", None),
            P(None, "mp"),
            P(None, "mp"),
            P("mp", None),
            P(),
        ),
        out_specs=(P("mp", "round", None), P()),
        check_vma=False,
    )
```

profile of v0, /device:TPU:1, one launch (start us, length us, event | category | flops | bytes accessed | tf_op | source)
XLA Modules:
  0.0 291.0 jit_solution(16656046799085090074)
XLA Ops:
  7.2 0.7 fusion.42
  7.9 0.8 copy.61
  8.7 18.4 %all-to-all-start.2 = ((bf16[128,1,2]{2,1,0:T(2,128)(2,1)}), bf16[128,1,2]{2,1,0:T(2,128)(2,1)S(1)}, u32[]{:S(2)}, u32[]{:S(2)}) async-start(bf16[128,1,2]{2,1,0:T(2,128)(2,1)} %copy.61), calls=%async_computation.2 | async-start | bytes 131072 | tf_op jit(solution)/shard_map/all_to_all | solution.py:79
  27.1 0.7 compare_select_fusion.2
  27.8 2.0 gather_fusion
  29.8 0.8 copy.95
  30.6 0.5 broadcast.153
  31.1 3.8 %reduce.2 = bf16[512,512]{1,0:T(8,128)(2,1)S(1)} reduce(bf16[512,1,512]{2,1,0:T(2,128)(2,1)S(1)} %bitcast.69, bf16[]{:T(256)} %broadcast.153), dimensions={1}, to_apply=%bitcast.66.reduce_sub_computation | reduce | bytes 1048578
  35.0 1.1 reshape.218
  36.1 2.4 all-to-all-done.2
  38.5 11.3 %all-to-all-start = ((bf16[128,2,1024]{2,1,0:T(2,128)(2,1)}), bf16[128,2,1024]{2,1,0:T(2,128)(2,1)S(1)}, u32[]{:S(2)}, u32[]{:S(2)}) async-start(bf16[128,2,1024]{2,1,0:T(2,128)(2,1)} %reshape.218), calls=%async_computation | async-start | bytes 1048576 | tf_op jit(solution)/shard_map/all_to_all | solution.py:56
  50.1 0.1 reshape.170
  50.2 0.1 squeeze.13
  50.4 0.2 compare_reduce_fusion
  50.6 0.1 gt.15
  50.8 19.6 %all-to-all-done = bf16[128,2,1024]{2,1,0:T(2,128)(2,1)S(1)} async-done(((bf16[128,2,1024]{2,1,0:T(2,128)(2,1)}), bf16[128,2,1024]{2,1,0:T(2,128)(2,1)S(1)}, u32[]{:S(2)}, u32[]{:S(2)}) %all-to-all-start) | async-done | bytes 524320 | tf_op jit(solution)/shard_map/all_to_all | solution.py:56
  70.4 0.4 reshape.219
  70.9 1.1 bitcast_convert_fusion
  72.0 0.1 fusion.9
  72.1 0.5 copy-done.7
  72.6 0.2 fusion.11
  72.8 0.2 copy-done.3
  73.0 0.3 convolution_convert_fusion.1
  73.3 0.2 copy-done.4
  73.5 0.3 convolution_convert_fusion.2
  74.0 0.1 copy.62
  74.1 1.5 gather_fusion.1
  75.6 1.5 gather_fusion.2
  77.0 6.3 %all-to-all-start.3 = ((bf16[128,2,128]{2,1,0:T(2,128)(2,1)}), bf16[128,2,128]{2,1,0:T(2,128)(2,1)}, u32[]{:S(2)}, u32[]{:S(2)}) async-start(bf16[128,2,128]{2,1,0:T(2,128)(2,1)} %bitcast.12), calls=%async_computation.3 | async-start | bytes 131072 | tf_op jit(solution)/shard_map/all_to_all | solution.py:76
  83.3 1.5 fusion.55
  84.8 1.0 convolution_convert_fusion
  85.8 1.0 copy.63
  86.8 1.5 gather_fusion.3
  88.3 5.8 %all-to-all-done.3 = bf16[128,2,128]{2,1,0:T(2,128)(2,1)} async-done(((bf16[128,2,128]{2,1,0:T(2,128)(2,1)}), bf16[128,2,128]{2,1,0:T(2,128)(2,1)}, u32[]{:S(2)}, u32[]{:S(2)}) %all-to-all-start.3) | async-done | bytes 65568 | tf_op jit(solution)/shard_map/all_to_all | solution.py:76
  94.1 8.0 %all-to-all-start.4 = ((bf16[128,2,128]{2,1,0:T(2,128)(2,1)}), bf16[128,2,128]{2,1,0:T(2,128)(2,1)}, u32[]{:S(2)}, u32[]{:S(2)}) async-start(bf16[128,2,128]{2,1,0:T(2,128)(2,1)} %bitcast.78), calls=%async_computation.4 | async-start | bytes 131072 | tf_op jit(solution)/shard_map/all_to_all | solution.py:77
  102.1 1.7 fusion.49
  103.9 0.9 reshape.151
  104.8 8.5 %all-to-all-done.4 = bf16[128,2,128]{2,1,0:T(2,128)(2,1)} async-done(((bf16[128,2,128]{2,1,0:T(2,128)(2,1)}), bf16[128,2,128]{2,1,0:T(2,128)(2,1)}, u32[]{:S(2)}, u32[]{:S(2)}) %all-to-all-start.4) | async-done | bytes 65568 | tf_op jit(solution)/shard_map/all_to_all | solution.py:77
  113.3 6.9 %all-to-all-start.1 = ((bf16[128,2,128]{2,1,0:T(2,128)(2,1)}), bf16[128,2,128]{2,1,0:T(2,128)(2,1)}, u32[]{:S(2)}, u32[]{:S(2)}) async-start(bf16[128,2,128]{2,1,0:T(2,128)(2,1)} %bitcast.76), calls=%async_computation.1 | async-start | bytes 131072 | tf_op jit(solution)/shard_map/all_to_all | solution.py:78
  120.2 1.6 reshape.152
  121.8 1.9 fusion.6
  123.7 1.2 fusion.50
  124.9 6.7 %all-to-all-done.1 = bf16[128,2,128]{2,1,0:T(2,128)(2,1)} async-done(((bf16[128,2,128]{2,1,0:T(2,128)(2,1)}), bf16[128,2,128]{2,1,0:T(2,128)(2,1)}, u32[]{:S(2)}, u32[]{:S(2)}) %all-to-all-start.1) | async-done | bytes 65568 | tf_op jit(solution)/shard_map/all_to_all | solution.py:78
  131.6 0.9 reshape.150
  132.6 2.1 fusion.7
  134.7 1.0 copy.68
  135.6 0.7 convert_element_type.92
  136.4 7.4 %all-to-all-start.5 = ((bf16[128,2,128]{2,1,0:T(2,128)(2,1)}), bf16[128,2,128]{2,1,0:T(2,128)(2,1)S(1)}, u32[]{:S(2)}, u32[]{:S(2)}) async-start(bf16[128,2,128]{2,1,0:T(2,128)(2,1)} %convert_element_type.92), calls=%async_computation.5 | async-start | bytes 131072 | tf_op jit(solution)/shard_map/all_to_all | solution.py:88
  143.8 2.7 fusion.18
  146.5 1.1 copy.69
  147.6 7.6 %all-to-all-done.5 = bf16[128,2,128]{2,1,0:T(2,128)(2,1)S(1)} async-done(((bf16[128,2,128]{2,1,0:T(2,128)(2,1)}), bf16[128,2,128]{2,1,0:T(2,128)(2,1)S(1)}, u32[]{:S(2)}, u32[]{:S(2)}) %all-to-all-start.5) | async-done | bytes 65568 | tf_op jit(solution)/shard_map/all_to_all | solution.py:88
  155.2 2.0 scatter_custom_fusion
  157.2 2.2 fusion.28
  159.4 3.3 %convolution_add_fusion = f32[512,512]{1,0:T(8,128)} fusion(f32[512,512]{1,0:T(8,128)} %fusion.28, bf16[512,512]{1,0:T(8,128)(2,1)} %param.24, bf16[512,512]{1,0:T(8,128)(2,1)S(1)} %fusion.11, bf16[512,512]{1,0:T(8,128)(2,1)} %param.23, f32[512,512]{1,0:T(8,128)S(1)} %fusion.55), kind=kOutput, calls=%fused_computation.12 | convolution fusion | flops 538705920 | bytes 4718592 | tf_op jit(solution)/shard_map/dot_general | solution.py:108
  162.8 0.7 copy-done.2
  163.5 0.1 copy.70
  163.6 0.8 compare_select_fusion.5
  164.4 0.6 gather_fusion.4
  165.1 0.3 constant_dynamic-slice_fusion
  165.3 18.2 %reduce-scatter.2.cloned.1.call-done = f32[128,512]{1,0:T(8,128)} async-done(((f32[512,512]{1,0:T(8,128)}), f32[128,512]{1,0:T(8,128)}) %reduce-scatter.2.cloned.1.call-update) | async-done | bytes 262160 | tf_op jit(solution)/shard_map/reduce_scatter | solution.py:107
  183.6 1.0 fusion.20
  184.7 0.2 fusion.38
  184.9 98.6 %psum.7 = f32[16,512]{1,0:T(8,128)S(1)} all-reduce(f32[16,512]{1,0:T(8,128)S(1)} %fusion.38), channel_id=1, replica_groups=mesh['round'=128,'mp'=4] {'round','mp'}, use_global_device_ids=true, to_apply=%region_8.9 | all-reduce | flops 8192 | bytes 65536 | tf_op jit(solution)/shard_map/psum | solution.py:123
  283.5 0.7 fusion.8
  (28 shorter events, 0.7 us)
Async XLA Ops:
  7.2 20.7 %copy-start = (bf16[1,512,512]{2,1,0:T(8,128)(2,1)S(1)}, bf16[1,512,512]{2,1,0:T(8,128)(2,1)}, u32[]{:S(2)}) copy-start(bf16[1,512,512]{2,1,0:T(8,128)(2,1)} %param.13) | copy-start | bytes 1572868
  8.7 29.8 %all-to-all-start.2 = ((bf16[128,1,2]{2,1,0:T(2,128)(2,1)}), bf16[128,1,2]{2,1,0:T(2,128)(2,1)S(1)}, u32[]{:S(2)}, u32[]{:S(2)}) async-start(bf16[128,1,2]{2,1,0:T(2,128)(2,1)} %copy.61), calls=%async_computation.2 | async-start | bytes 131072 | tf_op jit(solution)/shard_map/all_to_all | solution.py:79
  35.0 14.9 %copy-start.6 = (s32[1,128,2]{1,2,0:T(2,128)S(1)}, s32[1,128,2]{1,2,0:T(2,128)}, u32[]{:S(2)}) copy-start(s32[1,128,2]{1,2,0:T(2,128)} %param.15) | copy-start | bytes 3076
  38.5 31.9 %all-to-all-start = ((bf16[128,2,1024]{2,1,0:T(2,128)(2,1)}), bf16[128,2,1024]{2,1,0:T(2,128)(2,1)S(1)}, u32[]{:S(2)}, u32[]{:S(2)}) async-start(bf16[128,2,1024]{2,1,0:T(2,128)(2,1)} %reshape.218), calls=%async_computation | async-start | bytes 1048576 | tf_op jit(solution)/shard_map/all_to_all | solution.py:56
  71.9 0.7 copy-start.7
  72.1 0.9 copy-start.3
  72.6 0.9 copy-start.4
  77.0 17.0 %all-to-all-start.3 = ((bf16[128,2,128]{2,1,0:T(2,128)(2,1)}), bf16[128,2,128]{2,1,0:T(2,128)(2,1)}, u32[]{:S(2)}, u32[]{:S(2)}) async-start(bf16[128,2,128]{2,1,0:T(2,128)(2,1)} %bitcast.12), calls=%async_computation.3 | async-start | bytes 131072 | tf_op jit(solution)/shard_map/all_to_all | solution.py:76
  83.3 1.5 copy-start.5
  94.1 19.2 %all-to-all-start.4 = ((bf16[128,2,128]{2,1,0:T(2,128)(2,1)}), bf16[128,2,128]{2,1,0:T(2,128)(2,1)}, u32[]{:S(2)}, u32[]{:S(2)}) async-start(bf16[128,2,128]{2,1,0:T(2,128)(2,1)} %bitcast.78), calls=%async_computation.4 | async-start | bytes 131072 | tf_op jit(solution)/shard_map/all_to_all | solution.py:77
  113.3 18.3 %all-to-all-start.1 = ((bf16[128,2,128]{2,1,0:T(2,128)(2,1)}), bf16[128,2,128]{2,1,0:T(2,128)(2,1)}, u32[]{:S(2)}, u32[]{:S(2)}) async-start(bf16[128,2,128]{2,1,0:T(2,128)(2,1)} %bitcast.76), calls=%async_computation.1 | async-start | bytes 131072 | tf_op jit(solution)/shard_map/all_to_all | solution.py:78
  136.4 18.8 %all-to-all-start.5 = ((bf16[128,2,128]{2,1,0:T(2,128)(2,1)}), bf16[128,2,128]{2,1,0:T(2,128)(2,1)S(1)}, u32[]{:S(2)}, u32[]{:S(2)}) async-start(bf16[128,2,128]{2,1,0:T(2,128)(2,1)} %convert_element_type.92), calls=%async_computation.5 | async-start | bytes 131072 | tf_op jit(solution)/shard_map/all_to_all | solution.py:88
  143.8 39.8 %reduce-scatter.2.cloned.1.call-start = ((), (), s32[]{:S(2)}) async-start(), calls=%async_computation.7 | async-start | bytes 1310720 | tf_op jit(solution)/shard_map/reduce_scatter | solution.py:107
  162.7 0.8 copy-start.2
  163.5 120.0 %copy-start.8 = (f32[512]{0:T(512)S(1)}, f32[512]{0:T(512)}, u32[]{:S(2)}) copy-start(f32[512]{0:T(512)} %param.25) | copy-start | bytes 6148
  184.6 99.6 %copy-start.1 = (bf16[32,4,512]{2,1,0:T(4,128)(2,1)}, bf16[32,4,512]{2,1,0:T(4,128)(2,1)S(1)}, u32[]{:S(2)}) copy-start(bf16[32,4,512]{2,1,0:T(4,128)(2,1)S(1)} %reshape.153) | copy-start | bytes 393220
Sparse Core Ops, SparseCore 0:
  162.9 20.6 reduce-scatter.1
where the time goes:
time: 292 us; the launch traced here: 291 us
  blocking collectives  98.6 us (34%)
  waiting for transfers between devices  68.8 us (24%)
  starting transfers between devices  58.4 us (20%)
  local copies, waits for them, and re-layouts  20.8 us (7%)
  matrix products  19.2 us (7%)
  between operations  14.4 us (5%)
  other arithmetic  10.9 us (4%)
    psum x1, blocking collectives, shards(): pooled = lax.psum(partial_sum, ('round', 'mp'))  98.6 us
    all_to_all x1, waiting for transfers between devices, shards(): lax.all_to_all(permuted, 'round', split_axis=1, concat_axis=0, tiled=True)  19.6 us
    all_to_all x1, starting transfers between devices, shards(): lax.all_to_all(live_slot.astype(jnp.bfloat16), 'round', split_axis=0, con...  18.4 us
    reduce_scatter x1, waiting for transfers between devices, shards(): lax.psum_scatter(attn_part + jnp.dot(hidden, w_down, preferred_element_ty...  18.2 us
    all_to_all x1, starting transfers between devices, shards(): lax.all_to_all(permuted, 'round', split_axis=1, concat_axis=0, tiled=True)  11.3 us
    all_to_all x1, waiting for transfers between devices, shards(): lax.all_to_all(keys_all[safe_rows], 'round', split_axis=0, concat_axis=0,...  8.46 us
    all_to_all x1, starting transfers between devices, shards(): lax.all_to_all(keys_all[safe_rows], 'round', split_axis=0, concat_axis=0,...  8.03 us
    all_to_all x1, waiting for transfers between devices, shards(): lax.all_to_all(seam_attn.reshape(round_count, -1, head_width), 'round', s...  7.59 us
  transfers between devices with their start and end apart: 7, of which 7 were waited for; matrix products, arithmetic and copies ran while one was open for 10% of the time, Pallas kernels for 0%

commit v1 on v0

--- a/solution.py
+++ b/solution.py
@@ -120,7 +120,7 @@
     )
     support_count = round_count * jnp.sum(obs_mask.astype(jnp.float32), axis=1)
     divisor = jnp.sqrt(support_count)
-    pooled = lax.psum(partial_sum, ("round", "mp"))
+    pooled = lax.psum(lax.psum(partial_sum, "round"), "mp")
     obs_logits = jnp.dot(pooled, w_read, precision=lax.Precision.HIGHEST) / divisor
     return (tiles_out, obs_logits)
 

time: 292 us -> 703 us (2.41)
  blocking collectives: 98.6 us -> 503 us
    psum x1 -> x2, blocking collectives: 98.6 us -> 503 us  [shards(): pooled = lax.psum(lax.psum(partial_sum, 'round'), 'mp')]
  transfers between devices with their start and end apart: 7 -> 7, of which waited for: 7 -> 7; matrix products, arithmetic and copies ran while one was open for 10% -> 4% of each run, Pallas kernels for 0% -> 0%
where the time goes in v1:
time: 703 us; the launch traced here: 696 us
  blocking collectives  503 us (72%)
  waiting for transfers between devices  68.8 us (10%)
  starting transfers between devices  58.4 us (8%)
  local copies, waits for them, and re-layouts  20.8 us (3%)
  matrix products  19.2 us (3%)
  between operations  14.4 us (2%)
  other arithmetic  10.9 us (2%)
    psum x2, blocking collectives, shards(): pooled = lax.psum(lax.psum(partial_sum, 'round'), 'mp')  503 us
    all_to_all x1, waiting for transfers between devices, shards(): lax.all_to_all(permuted, 'round', split_axis=1, concat_axis=0, tiled=True)  19.6 us
    all_to_all x1, starting transfers between devices, shards(): lax.all_to_all(live_slot.astype(jnp.bfloat16), 'round', split_axis=0, con...  18.4 us
    reduce_scatter x1, waiting for transfers between devices, shards(): lax.psum_scatter(attn_part + jnp.dot(hidden, w_down, preferred_element_ty...  18.2 us
  transfers between devices with their start and end apart: 7, of which 7 were waited for; matrix products, arithmetic and copies ran while one was open for 4% of the time, Pallas kernels for 0%

profile of v1, /device:TPU:1, one launch (start us, length us, event | category | flops | bytes accessed | tf_op | source)
XLA Modules:
  0.0 695.7 jit_solution(7719618534248946246)
XLA Ops:
  7.2 0.7 fusion.42
  7.9 0.8 copy.61
  8.7 18.4 %all-to-all-start.2 = ((bf16[128,1,2]{2,1,0:T(2,128)(2,1)}), bf16[128,1,2]{2,1,0:T(2,128)(2,1)S(1)}, u32[]{:S(2)}, u32[]{:S(2)}) async-start(bf16[128,1,2]{2,1,0:T(2,128)(2,1)} %copy.61), calls=%async_computation.2 | async-start | bytes 131072 | tf_op jit(solution)/shard_map/all_to_all | solution.py:79
  27.1 0.7 compare_select_fusion.2
  27.8 2.0 gather_fusion
  29.8 0.8 copy.95
  30.6 0.5 broadcast.153
  31.1 3.8 reduce.2
  35.0 1.1 reshape.218
  36.1 2.4 all-to-all-done.2
  38.5 11.3 %all-to-all-start = ((bf16[128,2,1024]{2,1,0:T(2,128)(2,1)}), bf16[128,2,1024]{2,1,0:T(2,128)(2,1)S(1)}, u32[]{:S(2)}, u32[]{:S(2)}) async-start(bf16[128,2,1024]{2,1,0:T(2,128)(2,1)} %reshape.218), calls=%async_computation | async-start | bytes 1048576 | tf_op jit(solution)/shard_map/all_to_all | solution.py:56
  50.1 0.1 reshape.170
  50.2 0.1 squeeze.13
  50.4 0.2 compare_reduce_fusion
  50.6 0.1 gt.15
  50.8 19.6 %all-to-all-done = bf16[128,2,1024]{2,1,0:T(2,128)(2,1)S(1)} async-done(((bf16[128,2,1024]{2,1,0:T(2,128)(2,1)}), bf16[128,2,1024]{2,1,0:T(2,128)(2,1)S(1)}, u32[]{:S(2)}, u32[]{:S(2)}) %all-to-all-start) | async-done | bytes 524320 | tf_op jit(solution)/shard_map/all_to_all | solution.py:56
  70.4 0.4 reshape.219
  70.9 1.1 bitcast_convert_fusion
  72.0 0.1 fusion.9
  72.1 0.5 copy-done.7
  72.6 0.2 fusion.11
  72.8 0.2 copy-done.3
  73.0 0.3 convolution_convert_fusion.1
  73.3 0.2 copy-done.4
  73.5 0.3 convolution_convert_fusion.2
  74.0 0.1 copy.62
  74.1 1.5 gather_fusion.1
  75.6 1.5 gather_fusion.2
  77.0 6.3 all-to-all-start.3
  83.3 1.5 fusion.55
  84.8 1.0 convolution_convert_fusion
  85.8 1.0 copy.63
  86.8 1.5 gather_fusion.3
  88.3 5.8 all-to-all-done.3
  94.1 8.0 %all-to-all-start.4 = ((bf16[128,2,128]{2,1,0:T(2,128)(2,1)}), bf16[128,2,128]{2,1,0:T(2,128)(2,1)}, u32[]{:S(2)}, u32[]{:S(2)}) async-start(bf16[128,2,128]{2,1,0:T(2,128)(2,1)} %bitcast.78), calls=%async_computation.4 | async-start | bytes 131072 | tf_op jit(solution)/shard_map/all_to_all | solution.py:77
  102.1 1.7 fusion.49
  103.9 0.9 reshape.151
  104.8 8.5 %all-to-all-done.4 = bf16[128,2,128]{2,1,0:T(2,128)(2,1)} async-done(((bf16[128,2,128]{2,1,0:T(2,128)(2,1)}), bf16[128,2,128]{2,1,0:T(2,128)(2,1)}, u32[]{:S(2)}, u32[]{:S(2)}) %all-to-all-start.4) | async-done | bytes 65568 | tf_op jit(solution)/shard_map/all_to_all | solution.py:77
  113.3 6.9 all-to-all-start.1
  120.2 1.6 reshape.152
  121.8 1.9 fusion.6
  123.7 1.2 fusion.50
  124.9 6.7 all-to-all-done.1
  131.6 0.9 reshape.150
  132.6 2.1 fusion.7
  134.7 1.0 copy.68
  135.6 0.7 convert_element_type.92
  136.4 7.4 %all-to-all-start.5 = ((bf16[128,2,128]{2,1,0:T(2,128)(2,1)}), bf16[128,2,128]{2,1,0:T(2,128)(2,1)S(1)}, u32[]{:S(2)}, u32[]{:S(2)}) async-start(bf16[128,2,128]{2,1,0:T(2,128)(2,1)} %convert_element_type.92), calls=%async_computation.5 | async-start | bytes 131072 | tf_op jit(solution)/shard_map/all_to_all | solution.py:88
  143.8 2.7 fusion.18
  146.5 1.1 copy.69
  147.6 7.6 %all-to-all-done.5 = bf16[128,2,128]{2,1,0:T(2,128)(2,1)S(1)} async-done(((bf16[128,2,128]{2,1,0:T(2,128)(2,1)}), bf16[128,2,128]{2,1,0:T(2,128)(2,1)S(1)}, u32[]{:S(2)}, u32[]{:S(2)}) %all-to-all-start.5) | async-done | bytes 65568 | tf_op jit(solution)/shard_map/all_to_all | solution.py:88
  155.2 2.0 scatter_custom_fusion
  157.2 2.2 fusion.28
  159.4 3.3 convolution_add_fusion
  162.8 0.7 copy-done.2
  163.6 0.8 compare_select_fusion.5
  164.4 0.6 gather_fusion.4
  165.1 0.3 constant_dynamic-slice_fusion
  165.3 18.2 %reduce-scatter.2.cloned.1.call-done = f32[128,512]{1,0:T(8,128)} async-done(((f32[512,512]{1,0:T(8,128)}), f32[128,512]{1,0:T(8,128)}) %reduce-scatter.2.cloned.1.call-update) | async-done | bytes 262160 | tf_op jit(solution)/shard_map/reduce_scatter | solution.py:107
  183.6 1.0 fusion.20
  184.7 0.2 fusion.38
  184.9 491.7 %psum.14 = f32[16,512]{1,0:T(8,128)S(1)} all-reduce(f32[16,512]{1,0:T(8,128)S(1)} %fusion.38), channel_id=1, replica_groups=mesh['round'=128,'mp'=4] {'round'}, use_global_device_ids=true, to_apply=%region_8.9 | all-reduce | flops 8192 | bytes 65536 | tf_op jit(solution)/shard_map/psum | solution.py:123
  676.6 11.5 %psum.15 = f32[16,512]{1,0:T(8,128)S(1)} all-reduce(f32[16,512]{1,0:T(8,128)S(1)} %psum.14), channel_id=1, replica_groups=mesh['round'=128,'mp'=4] {'mp'}, use_global_device_ids=true, to_apply=%region_9.10 | all-reduce | flops 8192 | bytes 65536 | tf_op jit(solution)/shard_map/psum | solution.py:123
  688.2 0.7 fusion.8
  (29 shorter events, 0.8 us)
Async XLA Ops:
  7.2 20.7 %copy-start = (bf16[1,512,512]{2,1,0:T(8,128)(2,1)S(1)}, bf16[1,512,512]{2,1,0:T(8,128)(2,1)}, u32[]{:S(2)}) copy-start(bf16[1,512,512]{2,1,0:T(8,128)(2,1)} %param.13) | copy-start | bytes 1572868
  8.7 29.8 %all-to-all-start.2 = ((bf16[128,1,2]{2,1,0:T(2,128)(2,1)}), bf16[128,1,2]{2,1,0:T(2,128)(2,1)S(1)}, u32[]{:S(2)}, u32[]{:S(2)}) async-start(bf16[128,1,2]{2,1,0:T(2,128)(2,1)} %copy.61), calls=%async_computation.2 | async-start | bytes 131072 | tf_op jit(solution)/shard_map/all_to_all | solution.py:79
  35.0 14.9 %copy-start.6 = (s32[1,128,2]{1,2,0:T(2,128)S(1)}, s32[1,128,2]{1,2,0:T(2,128)}, u32[]{:S(2)}) copy-start(s32[1,128,2]{1,2,0:T(2,128)} %param.15) | copy-start | bytes 3076
  38.5 31.9 %all-to-all-start = ((bf16[128,2,1024]{2,1,0:T(2,128)(2,1)}), bf16[128,2,1024]{2,1,0:T(2,128)(2,1)S(1)}, u32[]{:S(2)}, u32[]{:S(2)}) async-start(bf16[128,2,1024]{2,1,0:T(2,128)(2,1)} %reshape.218), calls=%async_computation | async-start | bytes 1048576 | tf_op jit(solution)/shard_map/all_to_all | solution.py:56
  71.9 0.7 copy-start.7
  72.1 0.9 copy-start.3
  72.6 0.9 copy-start.4
  77.0 17.0 %all-to-all-start.3 = ((bf16[128,2,128]{2,1,0:T(2,128)(2,1)}), bf16[128,2,128]{2,1,0:T(2,128)(2,1)}, u32[]{:S(2)}, u32[]{:S(2)}) async-start(bf16[128,2,128]{2,1,0:T(2,128)(2,1)} %bitcast.12), calls=%async_computation.3 | async-start | bytes 131072 | tf_op jit(solution)/shard_map/all_to_all | solution.py:76
  83.3 1.5 copy-start.5
  94.1 19.2 %all-to-all-start.4 = ((bf16[128,2,128]{2,1,0:T(2,128)(2,1)}), bf16[128,2,128]{2,1,0:T(2,128)(2,1)}, u32[]{:S(2)}, u32[]{:S(2)}) async-start(bf16[128,2,128]{2,1,0:T(2,128)(2,1)} %bitcast.78), calls=%async_computation.4 | async-start | bytes 131072 | tf_op jit(solution)/shard_map/all_to_all | solution.py:77
  113.3 18.3 %all-to-all-start.1 = ((bf16[128,2,128]{2,1,0:T(2,128)(2,1)}), bf16[128,2,128]{2,1,0:T(2,128)(2,1)}, u32[]{:S(2)}, u32[]{:S(2)}) async-start(bf16[128,2,128]{2,1,0:T(2,128)(2,1)} %bitcast.76), calls=%async_computation.1 | async-start | bytes 131072 | tf_op jit(solution)/shard_map/all_to_all | solution.py:78
  136.4 18.8 %all-to-all-start.5 = ((bf16[128,2,128]{2,1,0:T(2,128)(2,1)}), bf16[128,2,128]{2,1,0:T(2,128)(2,1)S(1)}, u32[]{:S(2)}, u32[]{:S(2)}) async-start(bf16[128,2,128]{2,1,0:T(2,128)(2,1)} %convert_element_type.92), calls=%async_computation.5 | async-start | bytes 131072 | tf_op jit(solution)/shard_map/all_to_all | solution.py:88
  143.8 39.8 %reduce-scatter.2.cloned.1.call-start = ((), (), s32[]{:S(2)}) async-start(), calls=%async_computation.7 | async-start | bytes 1310720 | tf_op jit(solution)/shard_map/reduce_scatter | solution.py:107
  162.7 0.8 copy-start.2
  163.5 524.7 %copy-start.8 = (f32[512]{0:T(512)S(1)}, f32[512]{0:T(512)}, u32[]{:S(2)}) copy-start(f32[512]{0:T(512)} %param.25) | copy-start | bytes 6148
  184.6 504.3 %copy-start.1 = (bf16[32,4,512]{2,1,0:T(4,128)(2,1)}, bf16[32,4,512]{2,1,0:T(4,128)(2,1)S(1)}, u32[]{:S(2)}) copy-start(bf16[32,4,512]{2,1,0:T(4,128)(2,1)S(1)} %reshape.153) | copy-start | bytes 393220
Sparse Core Ops, SparseCore 0:
  162.9 20.6 reduce-scatter.1
